TPU v7x, 256 devices: a whole 4x4x8 slice. The times are simulated.
256 devices in a mesh: dp: 64 (over z, x, core), tensor: 4 (over y).
Axes of the slice: x: 4, y: 4, z: 8, core: 2. Of those that a mesh axis runs over, the one named last changes fastest.
Arguments:
- tokens: bfloat16 [24576, 8192], P('dp', 'tensor'), may hold values from -600 to 600
- norm_scale_vector: bfloat16 [8192], P('tensor'), may hold values from 0.5 to 2
- gate_matrix: bfloat16 [8192, 2048], P('dp', 'tensor'), may hold values from -0.0625 to 0.0625
- up_matrix: bfloat16 [8192, 2048], P('dp', 'tensor'), may hold values from -0.0625 to 0.0625
- adapter_down_factors: bfloat16 [64, 8192, 256], P('dp', 'tensor'), may hold values from -0.0625 to 0.0625
- adapter_up_factors: bfloat16 [64, 2, 128, 2048], P('dp', None, None, 'tensor'), may hold values from -0.5 to 0.5
- row_judges: int32 [24576, 1], P('dp'), may hold values from 0 to 63; in each aligned block of 384 rows (0 to 383, 384 to 767, ...) at most 12 rows name the same one
Outputs:
- hidden: bfloat16 [24576, 2048], P('dp', 'tensor')
Inputs may be any that keep to these rules, and one draw needn't show every extreme that they name: `row_judges`: among the 384 rows of one index of dp no judge is named more than 12 times, and on some index some judge is named exactly 12 times.
All inputs are finite; a program needn't handle non-finite values.
Results may differ from a plain program's by a relative error of at most 0.0063.
Values may be sent and summed in bfloat16 or wider, within the bound.
No kernel may reach another device: no remote copies, remote signals or barrier semaphores. Data moves between devices by JAX's collectives and lax.ppermute only.
A program may use at most 128 MiB of HBM per device.

v0:
```python
import jax
import jax.numpy as jnp
from jax import lax
from jax.sharding import PartitionSpec as P

EPSILON = 1e-06
ADAPTER_SCALE = 0.5


def body(
    tokens,
    norm_scale_vector,
    gate_matrix,
    up_matrix,
    adapter_down_factors,
    adapter_up_factors,
    row_judges,
):
    row_count = tokens.shape[0]
    part_width = tokens.shape[1]
    owners = lax.axis_size("dp")
    capacity = 2 * row_count // owners
    column_span = gate_matrix.shape[1]
    narrow_projection = adapter_up_factors.shape[2]
    wide_tokens = tokens.astype(jnp.float32)
    square_sum = lax.psum(jnp.sum(wide_tokens * wide_tokens, axis=1), "tensor")
    factor = lax.rsqrt(square_sum / (part_width * lax.axis_size("tensor")) + EPSILON)
    normed_part = (wide_tokens * factor[:, None] * norm_scale_vector.astype(jnp.float32)).astype(
        jnp.bfloat16
    )
    normalized_input = lax.all_gather(normed_part, "tensor", axis=1, tiled=True)

    def add_piece(weight_piece):
        return jnp.dot(normalized_input, weight_piece, preferred_element_type=jnp.float32)

    gate_plain = add_piece(lax.all_gather(gate_matrix, "dp", axis=0, tiled=True))
    up_plain = add_piece(lax.all_gather(up_matrix, "dp", axis=0, tiled=True))
    labels = row_judges[:, 0]
    owner_ids = jnp.arange(owners, dtype=jnp.int32)
    matches = (labels[:, None] == owner_ids[None, :]).astype(jnp.int32)
    before = jnp.cumsum(matches, axis=0) - matches
    place_in = jnp.sum(before * matches, axis=1)
    slot_index = labels * capacity + place_in
    outgoing = (
        jnp.zeros((owners * capacity, part_width), jnp.bfloat16).at[slot_index].set(normed_part)
    )
    outgoing = outgoing.reshape(owners, capacity, part_width)
    judge_down_factor = adapter_down_factors[0]
    judge_up_factor = adapter_up_factors[0]
    partial_sums = jnp.einsum(
        "sid,dr->sir",
        lax.all_to_all(outgoing, "dp", split_axis=0, concat_axis=0, tiled=True),
        judge_down_factor,
        preferred_element_type=jnp.float32,
    )
    down_projected = lax.psum(partial_sums, "tensor").astype(jnp.bfloat16)
    gate_adjustment = jnp.einsum(
        "sir,rf->sif",
        down_projected[:, :, :narrow_projection],
        judge_up_factor[0],
        preferred_element_type=jnp.float32,
    ).astype(jnp.bfloat16)
    up_adjustment = jnp.einsum(
        "sir,rf->sif",
        down_projected[:, :, narrow_projection:],
        judge_up_factor[1],
        preferred_element_type=jnp.float32,
    ).astype(jnp.bfloat16)
    deltas = jnp.concatenate([gate_adjustment, up_adjustment], axis=2)
    returned = lax.all_to_all(deltas, "dp", split_axis=0, concat_axis=0, tiled=True)
    returned_rows = returned.reshape(owners * capacity, 2 * column_span)
    judge_adjustments = returned_rows[slot_index]
    gate_combined = gate_plain + ADAPTER_SCALE * judge_adjustments[:, :column_span].astype(
        jnp.float32
    )
    up_combined = up_plain + ADAPTER_SCALE * judge_adjustments[:, column_span:].astype(jnp.float32)
    return (jax.nn.silu(gate_combined) * up_combined).astype(jnp.bfloat16)


def solution(mesh):
    placed = (
        P("dp", "tensor"),
        P("tensor"),
        P("dp", "tensor"),
        P("dp", "tensor"),
        P("dp", "tensor", None),
        P("dp", None, None, "tensor"),
        P("dp", None),
    )
    return jax.shard_map(
        body, mesh=mesh, in_specs=placed, out_specs=P("dp", "tensor"), check_vma=False
    )
```

profile of v0, /device:TPU:1, one launch (start us, length us, event | category | flops | bytes accessed | tf_op | source)
XLA Modules:
  0.0 289.8 jit_solution(4303549950230186500)
XLA Ops:
  6.5 0.0 copy-start
  6.5 0.8 convert_element_type.35
  7.3 1.8 fusion
  9.1 9.7 %psum.14 = f32[384]{0:T(512)S(1)} all-reduce(f32[384]{0:T(512)S(1)} %fusion), channel_id=1, replica_groups=mesh['dp'=64,'tensor'=4] {'tensor'}, use_global_device_ids=true, to_apply=%region_1.0 | all-reduce | flops 384 | bytes 3072 | tf_op jit(solution)/shard_map/psum | solution.py:26
  18.8 3.0 %fusion.2 = bf16[384,2048]{1,0:T(8,128)(2,1)} fusion(bf16[384,2048]{1,0:T(8,128)(2,1)} %param.7, f32[2048]{0:T(1024)S(1)} %convert_element_type.35, f32[384]{0:T(512)S(1)} %add_rsqrt_fusion), kind=kLoop, calls=%fused_computation.6 | loop fusion | flops 3145728 | bytes 3155456 | tf_op jit(solution)/shard_map/convert_element_type | solution.py:28
  21.8 0.0 all-gather.4.cloned.1.call-update
  21.8 0.0 all-gather.6.cloned.1.call-start
  21.9 0.7 all-gather.6.cloned.1.call-update
  22.6 0.0 all-gather.8.cloned.1.call-start
  22.6 0.7 all-gather.8.cloned.1.call-update
  23.4 0.9 reduce-window.6
  24.3 0.2 slice_reduce_fusion
  24.5 0.1 fusion.18
  24.7 5.2 %scatter_custom_fusion = bf16[768,2048]{1,0:T(8,128)(2,1)} fusion(s32[384]{0:T(512)S(1)} %fusion.20, bf16[]{:T(256)} %constant.6.clone.1, bf16[384,2048]{1,0:T(8,128)(2,1)S(1)} %copy-done.1, f32[2048]{0:T(1024)S(1)} %convert_element_type.35, f32[384]{0:T(512)S(1)} %add_rsqrt_fusion), kind=kCustom, calls=%fused_computation.10 | custom fusion | flops 3145728 | bytes 4728834 | tf_op jit(solution)/shard_map/scatter | solution.py:45
  29.9 6.1 %reshape.30 = bf16[64,12,2048]{2,1,0:T(8,128)(2,1)} reshape(bf16[768,2048]{1,0:T(8,128)(2,1)} %scatter_custom_fusion) | data formatting | bytes 6291456 | tf_op jit(solution)/shard_map/reshape | solution.py:47
  36.0 113.8 %all_to_all.10 = bf16[64,12,2048]{2,1,0:T(8,128)(2,1)S(1)} all-to-all(bf16[64,12,2048]{2,1,0:T(8,128)(2,1)} %reshape.30), channel_id=1, replica_groups=mesh['dp'=64,'tensor'=4] {'dp'}, dimensions={0} | all-to-all | bytes 6291456 | tf_op jit(solution)/shard_map/all_to_all | solution.py:52
  149.8 0.0 copy-done
  149.8 3.5 %fusion.3 = f32[64,12,256]{2,0,1:T(8,128)S(1)} fusion(bf16[64,12,2048]{2,1,0:T(8,128)(2,1)S(1)} %all_to_all.10, bf16[1,2048,256]{2,1,0:T(8,128)(2,1)S(1)} %copy-done), kind=kOutput, calls=%fused_computation.7 | convolution fusion | flops 805306368 | bytes 4980736 | tf_op jit(solution)/shard_map/sid,dr->sir/dot_general | solution.py:50
  153.3 20.8 %all-reduce.1 = bf16[64,12,256]{2,0,1:T(8,128)(2,1)S(1)} all-reduce(f32[64,12,256]{2,0,1:T(8,128)S(1)} %fusion.3), channel_id=1, replica_groups=mesh['dp'=64,'tensor'=4] {'tensor'}, use_global_device_ids=true, to_apply=%region_6.7 | all-reduce | flops 196608 | bytes 1179648 | tf_op jit(solution)/shard_map/psum | solution.py:56
  174.1 0.3 convolution_convert_fusion
  174.5 0.3 convolution_convert_fusion.1
  174.8 0.2 pad_maximum_fusion
  175.0 2.3 copy.13
  177.3 11.8 %all-to-all-start.1 = ((bf16[64,12,1024]{2,1,0:T(8,128)(2,1)}), bf16[64,12,1024]{2,1,0:T(8,128)(2,1)}, u32[]{:S(2)}, u32[]{:S(2)}) async-start(bf16[64,12,1024]{2,1,0:T(8,128)(2,1)} %copy.13), calls=%async_computation.1 | async-start | bytes 4194304 | tf_op jit(solution)/shard_map/all_to_all | solution.py:70
  189.1 54.5 %all-to-all-done.1 = bf16[64,12,1024]{2,1,0:T(8,128)(2,1)} async-done(((bf16[64,12,1024]{2,1,0:T(8,128)(2,1)}), bf16[64,12,1024]{2,1,0:T(8,128)(2,1)}, u32[]{:S(2)}, u32[]{:S(2)}) %all-to-all-start.1) | async-done | bytes 1572896 | tf_op jit(solution)/shard_map/all_to_all | solution.py:70
  243.6 2.5 reshape.31
  246.1 2.1 gather_fusion
  248.2 0.0 all-gather.4.cloned.1.call-done
  248.3 0.0 all-gather.6.cloned.1.call-done
  248.3 8.0 %convolution_add_fusion.1 = f32[384,512]{1,0:T(8,128)S(1)} fusion(bf16[384,8192]{1,0:T(8,128)(2,1)} %all-gather.4.cloned.1.call-done, bf16[8192,512]{1,0:T(8,128)(2,1)} %all-gather.6.cloned.1.call-done, bf16[384,1024]{1,0:T(8,128)(2,1)S(1)} %gather_fusion), kind=kOutput, calls=%fused_computation.16 | convolution fusion | flops 3221815296 | bytes 15859712 | tf_op jit(solution)/shard_map/dot_general | solution.py:34
  256.3 17.6 %all-gather.8.cloned.1.call-done = bf16[8192,512]{1,0:T(8,128)(2,1)} async-done(((bf16[128,512]{1,0:T(8,128)(2,1)}), bf16[8192,512]{1,0:T(8,128)(2,1)}) %all-gather.8.cloned.1.call-update) | async-done | bytes 8388624 | tf_op jit(solution)/shard_map/all_gather | solution.py:37
  273.9 9.4 %fusion.8 = bf16[384,512]{1,0:T(8,128)(2,1)} fusion(bf16[384,8192]{1,0:T(8,128)(2,1)} %all-gather.4.cloned.1.call-done, bf16[8192,512]{1,0:T(8,128)(2,1)} %all-gather.8.cloned.1.call-done, f32[384,512]{1,0:T(8,128)S(1)} %convolution_add_fusion.1, bf16[384,1024]{1,0:T(8,128)(2,1)S(1)} %gather_fusion), kind=kOutput, calls=%fused_computation.17 | convolution fusion | flops 3222994944 | bytes 16252928 | tf_op jit(solution)/shard_map/dot_general | solution.py:34
  (13 shorter events, 0.1 us)
Async XLA Ops:
  6.5 143.3 %copy-start = (bf16[1,2048,256]{2,1,0:T(8,128)(2,1)S(1)}, bf16[1,2048,256]{2,1,0:T(8,128)(2,1)}, u32[]{:S(2)}) copy-start(bf16[1,2048,256]{2,1,0:T(8,128)(2,1)} %param.11) | copy-start | bytes 3145732
  6.5 241.7 %all-gather.4.cloned.1.call-start = ((), (), s32[]{:S(2)}) async-start(), calls=%async_computation.2 | async-start | bytes 7864320 | tf_op jit(solution)/shard_map/all_gather | solution.py:31
  7.3 16.0 %copy-start.3 = (s32[384,1]{0,1:T(1,128)S(1)}, s32[384,1]{0,1:T(1,128)}, u32[]{:S(2)}) copy-start(s32[384,1]{0,1:T(1,128)} %param.13) | copy-start | bytes 4612
  9.1 15.6 %copy-start.1 = (bf16[384,2048]{1,0:T(8,128)(2,1)S(1)}, bf16[384,2048]{1,0:T(8,128)(2,1)}, u32[]{:S(2)}) copy-start(bf16[384,2048]{1,0:T(8,128)(2,1)} %param.7) | copy-start | bytes 4718596
  21.8 226.4 %all-gather.6.cloned.1.call-start = ((), (), s32[]{:S(2)}) async-start(), calls=%async_computation.3 | async-start | bytes 8519680 | tf_op jit(solution)/shard_map/all_gather | solution.py:36
  22.6 251.3 %all-gather.8.cloned.1.call-start = ((), (), s32[]{:S(2)}) async-start(), calls=%async_computation.4 | async-start | bytes 8519680 | tf_op jit(solution)/shard_map/all_gather | solution.py:37
  149.8 24.3 %copy-start.2 = (bf16[1,2,128,512]{3,2,1,0:T(8,128)(2,1)S(1)}, bf16[1,2,128,512]{3,2,1,0:T(8,128)(2,1)}, u32[]{:S(2)}) copy-start(bf16[1,2,128,512]{3,2,1,0:T(8,128)(2,1)} %param.12) | copy-start | bytes 786436
  177.3 66.3 %all-to-all-start.1 = ((bf16[64,12,1024]{2,1,0:T(8,128)(2,1)}), bf16[64,12,1024]{2,1,0:T(8,128)(2,1)}, u32[]{:S(2)}, u32[]{:S(2)}) async-start(bf16[64,12,1024]{2,1,0:T(8,128)(2,1)} %copy.13), calls=%async_computation.1 | async-start | bytes 4194304 | tf_op jit(solution)/shard_map/all_to_all | solution.py:70
Sparse Core Ops, SparseCore 0:
  22.0 70.8 all-gather.3
  95.7 90.0 all-gather.5
  188.5 85.3 all-gather.7
where the time goes:
time: 290 us
  blocking collectives  144 us (50%)
  waiting for transfers between devices  73.5 us (25%)
  matrix products  21.6 us (7%)
  local copies, waits for them, and re-layouts  13.2 us (5%)
  between operations  13.2 us (5%)
  other arithmetic  12.1 us (4%)
  starting transfers between devices  11.9 us (4%)
    all_to_all x1, blocking collectives, body(): lax.all_to_all(outgoing, 'dp', split_axis=0, concat_axis=0, tiled=True)  114 us
    all_to_all x1, waiting for transfers between devices, body(): lax.all_to_all(deltas, 'dp', split_axis=0, concat_axis=0, tiled=True)  54.5 us
    psum x1, blocking collectives, body(): down_projected = lax.psum(partial_sums, 'tensor').astype(jnp.bfloat16)  20.8 us
    all_gather x1, waiting for transfers between devices, body(): up_plain = add_piece(lax.all_gather(up_matrix, 'dp', axis=0, tiled=True))  17.6 us
    dot_general x2, matrix products, add_piece(): jnp.dot(normalized_input, weight_piece, preferred_element_type=jnp.float32)  17.4 us
    all_to_all x1, starting transfers between devices, body(): lax.all_to_all(deltas, 'dp', split_axis=0, concat_axis=0, tiled=True)  11.8 us
    psum x1, blocking collectives, body(): square_sum = lax.psum(jnp.sum(wide_tokens * wide_tokens, axis=1), 'tensor')  9.69 us
    reshape x1, local copies, waits for them, and re-layouts, body(): outgoing = outgoing.reshape(owners, capacity, part_width)  6.07 us
  transfers between devices with their start and end apart: 4, of which 2 were waited for; matrix products, arithmetic and copies ran while one was open for 11% of the time, Pallas kernels for 0%

commit v1 on v0

--- a/solution.py
+++ b/solution.py
@@ -5,6 +5,11 @@
 
 EPSILON = 1e-06
 ADAPTER_SCALE = 0.5
+
+
+def gather_from_all(x, axis, dim):
+    copies = jnp.concatenate([x] * lax.axis_size(axis), axis=dim)
+    return lax.all_to_all(copies, axis, dim, dim, tiled=True)
 
 
 def body(
@@ -34,7 +39,7 @@
         return jnp.dot(normalized_input, weight_piece, preferred_element_type=jnp.float32)
 
     gate_plain = add_piece(lax.all_gather(gate_matrix, "dp", axis=0, tiled=True))
-    up_plain = add_piece(lax.all_gather(up_matrix, "dp", axis=0, tiled=True))
+    up_plain = add_piece(gather_from_all(up_matrix, "dp", 0))
     labels = row_judges[:, 0]
     owner_ids = jnp.arange(owners, dtype=jnp.int32)
     matches = (labels[:, None] == owner_ids[None, :]).astype(jnp.int32)

time: 290 us -> 453 us (1.56)
  waiting for transfers between devices: 73.5 us -> 277 us
  blocking collectives: 144 us -> 30 us
  local copies, waits for them, and re-layouts: 13.2 us -> 56.6 us
  starting transfers between devices: 11.9 us -> 33.9 us
    all_to_all x0 -> x2, waiting for transfers between devices: none -> 245 us  [the longest x1 170 us: gather_from_all(): return lax.all_to_all(copies, axis, dim, dim, tiled=True)]
    all_to_all x1 -> x0, blocking collectives: 114 us -> none  [body(): lax.all_to_all(outgoing, 'dp', split_axis=0, concat_axis=0, tiled=True)]
    unnamed x8 -> x71, local copies, waits for them, and re-layouts: 0.02 us -> 42.7 us
    all_to_all x1, waiting for transfers between devices: 54.5 us -> 31.9 us  [body(): lax.all_to_all(deltas, 'dp', split_axis=0, concat_axis=0, tiled=True)]
    all_to_all x0 -> x2, starting transfers between devices: none -> 21.8 us  [the longest x1 14.5 us: body(): lax.all_to_all(outgoing, 'dp', split_axis=0, concat_axis=0, tiled=True)]
    all_gather x1 -> x0, waiting for transfers between devices: 17.6 us -> none  [body(): up_plain = add_piece(lax.all_gather(up_matrix, 'dp', axis=0, tiled=True))]
  transfers between devices with their start and end apart: 4 -> 5, of which waited for: 2 -> 3; matrix products, arithmetic and copies ran while one was open for 11% -> 17% of each run, Pallas kernels for 0% -> 0%
where the time goes in v1:
time: 453 us; the launch traced here: 449 us
  waiting for transfers between devices  277 us (61%)
  local copies, waits for them, and re-layouts  56.6 us (12%)
  starting transfers between devices  33.9 us (7%)
  blocking collectives  30 us (7%)
  matrix products  23.6 us (5%)
  other arithmetic  14.2 us (3%)
  between operations  13.6 us (3%)
    all_to_all x1, waiting for transfers between devices, gather_from_all(): return lax.all_to_all(copies, axis, dim, dim, tiled=True)  170 us
    all_to_all x1, waiting for transfers between devices, body(): lax.all_to_all(outgoing, 'dp', split_axis=0, concat_axis=0, tiled=True)  74.2 us
    unnamed x71, local copies, waits for them, and re-layouts  42.7 us
    all_to_all x1, waiting for transfers between devices, body(): lax.all_to_all(deltas, 'dp', split_axis=0, concat_axis=0, tiled=True)  31.9 us
    psum x1, blocking collectives, body(): down_projected = lax.psum(partial_sums, 'tensor').astype(jnp.bfloat16)  20.4 us
    dot_general x2, matrix products, add_piece(): jnp.dot(normalized_input, weight_piece, preferred_element_type=jnp.float32)  17.2 us
    all_to_all x1, starting transfers between devices, body(): lax.all_to_all(outgoing, 'dp', split_axis=0, concat_axis=0, tiled=True)  14.5 us
    all_to_all x1, starting transfers between devices, body(): lax.all_to_all(deltas, 'dp', split_axis=0, concat_axis=0, tiled=True)  12.1 us
  transfers between devices with their start and end apart: 5, of which 3 were waited for; matrix products, arithmetic and copies ran while one was open for 17% of the time, Pallas kernels for 0%

profile of v1, /device:TPU:1, one launch (start us, length us, event | category | flops | bytes accessed | tf_op | source)
XLA Modules:
  0.0 449.1 jit_solution(13459869479907182494)
XLA Ops:
  6.5 1.9 fusion
  8.4 9.6 %psum.14 = f32[384]{0:T(512)S(1)} all-reduce(f32[384]{0:T(512)S(1)} %fusion), channel_id=1, replica_groups=mesh['dp'=64,'tensor'=4] {'tensor'}, use_global_device_ids=true, to_apply=%region_1.0 | all-reduce | flops 384 | bytes 3072 | tf_op jit(solution)/shard_map/psum | solution.py:31
  18.0 0.7 convert_element_type.35
  18.7 3.0 fusion.2
  21.7 0.7 reduce
  22.4 0.9 reduce-window.6
  23.7 0.7 fusion.20
  24.4 6.0 %scatter_custom_fusion = bf16[768,2048]{1,0:T(8,128)(2,1)} fusion(s32[384]{0:T(512)S(1)} %fusion.20, bf16[]{:T(256)} %constant.6.clone.1, bf16[384,2048]{1,0:T(8,128)(2,1)} %param.7, f32[2048]{0:T(1024)S(1)} %convert_element_type.35, f32[384]{0:T(512)S(1)} %add_rsqrt_fusion), kind=kCustom, calls=%fused_computation.10 | custom fusion | flops 3145728 | bytes 4728834 | tf_op jit(solution)/shard_map/scatter | solution.py:50
  30.4 6.1 %reshape.32 = bf16[64,12,2048]{2,1,0:T(8,128)(2,1)} reshape(bf16[768,2048]{1,0:T(8,128)(2,1)} %scatter_custom_fusion) | data formatting | bytes 6291456 | tf_op jit(solution)/shard_map/reshape | solution.py:52
  36.5 14.5 %all-to-all-start = ((bf16[64,12,2048]{2,1,0:T(8,128)(2,1)}), bf16[64,12,2048]{2,1,0:T(8,128)(2,1)}, u32[]{:S(2)}, u32[]{:S(2)}) async-start(bf16[64,12,2048]{2,1,0:T(8,128)(2,1)} %reshape.32), calls=%async_computation | async-start | bytes 8388608 | tf_op jit(solution)/shard_map/all_to_all | solution.py:57
  51.1 0.7 all-gather.5.cloned.1.call-update
  52.4 0.7 constant_dynamic-update-slice_fusion.62
  53.1 0.7 constant_dynamic-update-slice_fusion.61
  56.4 0.7 constant_dynamic-update-slice_fusion.56
  76.1 74.2 %all-to-all-done = bf16[64,12,2048]{2,1,0:T(8,128)(2,1)} async-done(((bf16[64,12,2048]{2,1,0:T(8,128)(2,1)}), bf16[64,12,2048]{2,1,0:T(8,128)(2,1)}, u32[]{:S(2)}, u32[]{:S(2)}) %all-to-all-start) | async-done | bytes 3145760 | tf_op jit(solution)/shard_map/all_to_all | solution.py:57
  150.3 5.6 %fusion.3 = f32[64,12,256]{2,0,1:T(8,128)S(1)} fusion(bf16[64,12,2048]{2,1,0:T(8,128)(2,1)} %all-to-all-done, bf16[1,2048,256]{2,1,0:T(8,128)(2,1)S(1)} %copy-done), kind=kOutput, calls=%fused_computation.7 | convolution fusion | flops 805306368 | bytes 4980736 | tf_op jit(solution)/shard_map/sid,dr->sir/dot_general | solution.py:55
  155.9 20.4 %all-reduce.1 = bf16[64,12,256]{2,0,1:T(8,128)(2,1)S(1)} all-reduce(f32[64,12,256]{2,0,1:T(8,128)S(1)} %fusion.3), channel_id=1, replica_groups=mesh['dp'=64,'tensor'=4] {'tensor'}, use_global_device_ids=true, to_apply=%region_6.7 | all-reduce | flops 196608 | bytes 1179648 | tf_op jit(solution)/shard_map/psum | solution.py:61
  177.3 2.3 copy.13
  179.6 12.1 %all-to-all-start.1 = ((bf16[64,12,1024]{2,1,0:T(8,128)(2,1)}), bf16[64,12,1024]{2,1,0:T(8,128)(2,1)S(1)}, u32[]{:S(2)}, u32[]{:S(2)}) async-start(bf16[64,12,1024]{2,1,0:T(8,128)(2,1)} %copy.13), calls=%async_computation.1 | async-start | bytes 4194304 | tf_op jit(solution)/shard_map/all_to_all | solution.py:75
  191.7 0.7 constant_dynamic-update-slice_fusion.26
  192.4 0.7 constant_dynamic-update-slice_fusion.25
  195.0 0.7 constant_dynamic-update-slice_fusion.21
  200.3 0.7 constant_dynamic-update-slice_fusion.13
  208.8 0.7 constant_dynamic-update-slice_fusion
  209.5 31.9 %all-to-all-done.1 = bf16[64,12,1024]{2,1,0:T(8,128)(2,1)S(1)} async-done(((bf16[64,12,1024]{2,1,0:T(8,128)(2,1)}), bf16[64,12,1024]{2,1,0:T(8,128)(2,1)S(1)}, u32[]{:S(2)}, u32[]{:S(2)}) %all-to-all-start.1) | async-done | bytes 1572896 | tf_op jit(solution)/shard_map/all_to_all | solution.py:75
  241.4 1.3 copy-done.2
  242.7 7.3 %all-to-all-start.2 = ((bf16[64,128,512]{2,1,0:T(8,128)(2,1)}), bf16[64,128,512]{2,1,0:T(8,128)(2,1)}, u32[]{:S(2)}, u32[]{:S(2)}) async-start(bf16[64,128,512]{2,1,0:T(8,128)(2,1)} %bitcast.7), calls=%async_computation.2 | async-start | bytes 16777216 | tf_op jit(solution)/shard_map/all_to_all | solution.py:12
  250.0 2.5 reshape.33
  252.5 2.1 gather_fusion
  254.6 7.8 %convolution_add_fusion.1 = f32[384,512]{1,0:T(8,128)S(1)} fusion(bf16[384,8192]{1,0:T(8,128)(2,1)} %all-gather.3.cloned.1.call-done, bf16[8192,512]{1,0:T(8,128)(2,1)} %all-gather.5.cloned.1.call-done, bf16[384,1024]{1,0:T(8,128)(2,1)S(1)} %gather_fusion), kind=kOutput, calls=%fused_computation.16 | convolution fusion | flops 3221815296 | bytes 15859712 | tf_op jit(solution)/shard_map/dot_general | solution.py:39
  262.4 170.4 %all-to-all-done.2 = bf16[64,128,512]{2,1,0:T(8,128)(2,1)} async-done(((bf16[64,128,512]{2,1,0:T(8,128)(2,1)}), bf16[64,128,512]{2,1,0:T(8,128)(2,1)}, u32[]{:S(2)}, u32[]{:S(2)}) %all-to-all-start.2) | async-done | bytes 8388640 | tf_op jit(solution)/shard_map/all_to_all | solution.py:12
  432.9 9.4 %fusion.8 = bf16[384,512]{1,0:T(8,128)(2,1)} fusion(bf16[384,8192]{1,0:T(8,128)(2,1)} %all-gather.3.cloned.1.call-done, bf16[8192,512]{1,0:T(8,128)(2,1)} %bitcast.8, f32[384,512]{1,0:T(8,128)S(1)} %convolution_add_fusion.1, bf16[384,1024]{1,0:T(8,128)(2,1)S(1)} %gather_fusion), kind=kOutput, calls=%fused_computation.17 | convolution fusion | flops 3222994944 | bytes 16252928 | tf_op jit(solution)/shard_map/dot_general | solution.py:39
  (77 shorter events, 38.1 us)
Async XLA Ops:
  6.5 143.8 %copy-start = (bf16[1,2048,256]{2,1,0:T(8,128)(2,1)S(1)}, bf16[1,2048,256]{2,1,0:T(8,128)(2,1)}, u32[]{:S(2)}) copy-start(bf16[1,2048,256]{2,1,0:T(8,128)(2,1)} %param.11) | copy-start | bytes 3145732
  6.5 248.1 %all-gather.3.cloned.1.call-start = ((), (), s32[]{:S(2)}) async-start(), calls=%async_computation.3 | async-start | bytes 7864320 | tf_op jit(solution)/shard_map/all_gather | solution.py:36
  30.4 21.4 %copy-start.1 = (bf16[128,512]{1,0:T(8,128)(2,1)S(1)}, bf16[128,512]{1,0:T(8,128)(2,1)}, u32[]{:S(2)}) copy-start(bf16[128,512]{1,0:T(8,128)(2,1)} %param.10) | copy-start | bytes 393220
  36.5 113.8 %all-to-all-start = ((bf16[64,12,2048]{2,1,0:T(8,128)(2,1)}), bf16[64,12,2048]{2,1,0:T(8,128)(2,1)}, u32[]{:S(2)}, u32[]{:S(2)}) async-start(bf16[64,12,2048]{2,1,0:T(8,128)(2,1)} %reshape.32), calls=%async_computation | async-start | bytes 8388608 | tf_op jit(solution)/shard_map/all_to_all | solution.py:57
  51.0 203.6 %all-gather.5.cloned.1.call-start = ((), (), s32[]{:S(2)}) async-start(), calls=%async_computation.4 | async-start | bytes 8519680 | tf_op jit(solution)/shard_map/all_gather | solution.py:41
  68.2 108.1 %copy-start.3 = (bf16[1,2,128,512]{3,2,1,0:T(8,128)(2,1)S(1)}, bf16[1,2,128,512]{3,2,1,0:T(8,128)(2,1)}, u32[]{:S(2)}) copy-start(bf16[1,2,128,512]{3,2,1,0:T(8,128)(2,1)} %param.12) | copy-start | bytes 786436
  179.6 61.8 %all-to-all-start.1 = ((bf16[64,12,1024]{2,1,0:T(8,128)(2,1)}), bf16[64,12,1024]{2,1,0:T(8,128)(2,1)S(1)}, u32[]{:S(2)}, u32[]{:S(2)}) async-start(bf16[64,12,1024]{2,1,0:T(8,128)(2,1)} %copy.13), calls=%async_computation.1 | async-start | bytes 4194304 | tf_op jit(solution)/shard_map/all_to_all | solution.py:75
  241.4 1.3 copy-start.2
  242.7 190.2 %all-to-all-start.2 = ((bf16[64,128,512]{2,1,0:T(8,128)(2,1)}), bf16[64,128,512]{2,1,0:T(8,128)(2,1)}, u32[]{:S(2)}, u32[]{:S(2)}) async-start(bf16[64,128,512]{2,1,0:T(8,128)(2,1)} %bitcast.7), calls=%async_computation.2 | async-start | bytes 16777216 | tf_op jit(solution)/shard_map/all_to_all | solution.py:12
Sparse Core Ops, SparseCore 0:
  21.8 70.8 all-gather.2
  95.5 93.2 all-gather.4
